TPU v7x, 1024 devices: a whole 8x8x8 slice. The times are simulated.
1024 devices in a mesh: row: 8 (over z_hi, core), col: 128 (over x, z_lo, y).
Axes of the slice: x: 8, y: 8, z: 8 (z_hi: 4, z_lo: 2; z = z_hi * 2 + z_lo), core: 2. Of those that a mesh axis runs over, the one named last changes fastest.
Arguments:
- vectors: float32 [16, 16, 1024, 256], P(None, 'row', 'col'), may hold values from -6 to 6
- leaf_order: int32 [16, 1024, 256], P('row', 'col'), may hold values from 0 to 255, each once within a row
- offsets: float32 [3, 16, 1024, 256], P(None, 'row', 'col'), may hold values from 0 to 1
- near_mask: int32 [9, 16, 1024], P(None, 'row', 'col'), may hold values 0 or 1
- far_mask: int32 [16, 16, 1024], P(None, 'row', 'col'), may hold values 0 or 1
- basis: float32 [16, 1024, 64, 256], P('row', 'col'), may hold values from -0.375 to 0.375
- transfer: float32 [16, 1024, 64, 64], P('row', 'col'), may hold values from -0.75 to 0.75
- coupling: float32 [16, 64, 64], replicated, may hold values from -0.25 to 0.25
- top_coupling: float32 [16, 64, 64], replicated, may hold values from -0.005859375 to 0.005859375
- cluster_owner: int32 [8, 128], P('row', 'col'), may hold values from 0 to 15
Outputs:
- product: float32 [16, 16, 1024, 256], P(None, 'row', 'col')
Inputs may be any that keep to these rules, and one draw needn't show every extreme that they name: `leaf_order`: each leaf's entries are a permutation of 0 to 255.
All inputs are finite; a program needn't handle non-finite values. No bound on the sum of `near_mask` or of `far_mask` on one device may be relied on, other than what follows from the above.
Results may differ from a plain program's by a relative error of at most 0.0003.
Values sent between devices are 32-bit elements; how exact they have to be, the bound alone decides.
A program may use at most 32 MiB of HBM per device.

v0:
```python
import math

import jax
import jax.numpy as jnp
from jax import lax
from jax.sharding import PartitionSpec as P

softening = 0.01


def extended(block, sides, width):
    for axis, dim in sides:
        count = lax.axis_size(axis)
        forward = [(i, i + 1) for i in range(count - 1)]
        backward = [(target, source) for source, target in forward]
        low = lax.ppermute(
            lax.slice_in_dim(block, block.shape[dim] - width, None, axis=dim), axis, forward
        )
        high = lax.ppermute(lax.slice_in_dim(block, 0, width, axis=dim), axis, backward)
        block = jnp.concatenate([low, block, high], axis=dim)
    return block


def far_offsets():
    found = []
    for down_step in range(-2, 3):
        for right_step in range(-2, 3):
            if max(abs(down_step), abs(right_step)) == 2:
                found.append((down_step, right_step))
    return found


def kernel_block(target, source):
    square = jnp.zeros(target.shape[1:] + (source.shape[-1],), jnp.float32)
    for comp in range(3):
        diff = target[comp][..., :, None] - source[comp][..., None, :]
        square = square + diff * diff
    return 1.0 / jnp.sqrt(square + softening)


def near_term(target, source, values, weight):
    tile = kernel_block(target, source) * weight.astype(jnp.float32)[:, :, None, None]
    return jnp.einsum("abij,sabj->sabi", tile, values, precision=lax.Precision.HIGHEST)


def near_field(pos, wide_pos, wide_vec, near_mask, edge):
    rows, cols, leaf = (pos.shape[1], pos.shape[2], pos.shape[3])
    total = jnp.zeros((wide_vec.shape[0], rows, cols, leaf), jnp.float32)
    for down_step in (-1, 0, 1):
        for right_step in (-1, 0, 1):
            slot = 3 * (down_step + 1) + right_step + 1
            first_row = edge + down_step
            first_col = edge + right_step
            source = wide_pos[:, first_row : first_row + rows, first_col : first_col + cols]
            values = wide_vec[:, first_row : first_row + rows, first_col : first_col + cols]
            total = total + near_term(pos, source, values, near_mask[slot])
    return total * (1.0 / (3.0 * math.sqrt(leaf)))


def inverse_order(order):
    flat = order.reshape(-1, order.shape[-1])
    iota = jnp.broadcast_to(jnp.arange(flat.shape[1], dtype=jnp.int32)[None, :], flat.shape)
    lines = jnp.broadcast_to(jnp.arange(flat.shape[0], dtype=jnp.int32)[:, None], flat.shape)
    inverse = jnp.zeros_like(flat).at[lines, flat].set(iota)
    return inverse.reshape(order.shape)


def on_device(
    vectors,
    leaf_order,
    offsets,
    near_mask,
    far_mask,
    basis,
    transfer,
    coupling,
    top_coupling,
    cluster_owner,
):
    hp = lax.Precision.HIGHEST
    rhs, rows, cols, leaf = vectors.shape
    rank = basis.shape[2]
    nodes_count = top_coupling.shape[0]
    packs = rank * rhs // leaf
    sorted_vec = jnp.take_along_axis(vectors, leaf_order[None], axis=3)
    row_first = (lax.axis_index("row") * rows).astype(jnp.float32)
    col_first = (lax.axis_index("col") * cols).astype(jnp.float32)
    row_pos = row_first + jnp.arange(rows, dtype=jnp.float32)[:, None, None] + offsets[0]
    col_pos = col_first + jnp.arange(cols, dtype=jnp.float32)[None, :, None] + offsets[1]
    pos = jnp.stack([row_pos, col_pos, 0.25 * offsets[2]], 0)
    coef = jnp.einsum("abkp,sabp->ksab", basis, sorted_vec, precision=hp)
    packed = jnp.transpose(coef.reshape(packs, leaf, rows, cols), (0, 2, 3, 1))
    near_block = jnp.concatenate([pos, sorted_vec], 0)
    near_wide = extended(near_block, (("row", 1), ("col", 2)), 1)
    near = near_field(pos, near_wide[:3], near_wide[3:], near_mask, 1)
    coef_wide = extended(packed, (("row", 1), ("col", 2)), 2)
    wide = jnp.transpose(coef_wide, (0, 3, 1, 2)).reshape(rank, rhs, rows + 4, cols + 4)
    far = jnp.zeros_like(coef)
    for slot, (down_step, right_step) in enumerate(far_offsets()):
        window = wide[
            :, :, 2 + down_step : 2 + down_step + rows, 2 + right_step : 2 + right_step + cols
        ]
        moved = jnp.einsum("jk,ksab->jsab", coupling[slot], window, precision=hp)
        far = far + moved * far_mask[slot].astype(jnp.float32)[None, None]
    cluster = jnp.einsum("abkj,ksab->js", transfer, coef, precision=hp)
    owner = cluster_owner[0, 0]
    nodes = jnp.arange(nodes_count, dtype=jnp.int32)
    keep = (nodes != owner).astype(jnp.float32)
    onehot = (nodes == owner).astype(jnp.float32)
    terms = (onehot[:, None, None] * cluster[None]).reshape(nodes_count, rank * rhs)
    top = lax.psum(terms, ("row", "col")).reshape(nodes_count, rank, rhs)
    table = top_coupling[(owner - nodes) % nodes_count]
    device_local = jnp.einsum("h,hjk,hks->js", keep, table, top, precision=hp)
    down = jnp.einsum("abkj,js->ksab", transfer, device_local, precision=hp)
    local = far + down
    result = near + jnp.einsum("abkp,ksab->sabp", basis, local, precision=hp)
    return jnp.take_along_axis(result, inverse_order(leaf_order)[None], axis=3)


def solution(mesh):
    in_specs = (
        P(None, "row", "col", None),
        P("row", "col", None),
        P(None, "row", "col", None),
        P(None, "row", "col"),
        P(None, "row", "col"),
        P("row", "col", None, None),
        P("row", "col", None, None),
        P(),
        P(),
        P("row", "col"),
    )
    out_specs = P(None, "row", "col", None)
    return jax.shard_map(
        on_device, mesh=mesh, in_specs=in_specs, out_specs=out_specs, check_vma=False
    )
```

profile of v0, /device:TPU:1, one launch (start us, length us, event | category | flops | bytes accessed | tf_op | source)
XLA Modules:
  0.0 517.4 jit_solution(5638527574410553766)
XLA Ops:
  8.1 1.6 copy.57
  9.7 50.9 %gather_fusion.1 = f32[4096,16]{1,0:T(8,128)} fusion(f32[16,2,8,256]{0,3,2,1:T(8,128)S(1)} %copy.57, s32[4096]{0:T(1024)S(1)} %bitcast.307), kind=kCustom, calls=%fused_computation.clone | custom fusion | bytes 573440 | tf_op jit(solution)/shard_map/jit(take_along_axis)/gather | solution.py:85
  60.6 2.2 copy.59
  64.4 9.1 %collective-permute-start.4 = (f32[4,2,8,256]{3,0,2,1:T(4,128)S(1)}, f32[4,2,8,256]{3,0,2,1:T(4,128)S(1)}, u32[]{:S(2)}, u32[]{:S(2)}) collective-permute-start(f32[4,2,8,256]{3,0,2,1:T(4,128)S(1)} %bitcast.310), channel_id=1, source_target_pairs={{0,128},{128,256},{256,384},{384,512},{512,640},{640,768},{768,896... | collective-permute-start | bytes 196616 | tf_op jit(solution)/shard_map/ppermute | solution.py:16
  73.5 8.3 %collective-permute-start.5 = (f32[4,2,8,256]{3,0,2,1:T(4,128)S(1)}, f32[4,2,8,256]{3,0,2,1:T(4,128)S(1)}, u32[]{:S(2)}, u32[]{:S(2)}) collective-permute-start(f32[4,2,8,256]{3,0,2,1:T(4,128)S(1)} %bitcast.311), channel_id=1, source_target_pairs={{128,0},{256,128},{384,256},{512,384},{640,512},{768,640},{896,768... | collective-permute-start | bytes 196616 | tf_op jit(solution)/shard_map/ppermute | solution.py:19
  85.3 1.9 collective-permute-start
  87.3 3.1 collective-permute-start.1
  90.7 15.5 %scatter_custom_fusion = s32[4096]{0:T(1024)S(1)} fusion(s32[4096]{0:T(1024)S(1)} %bitcast.349, s32[4096]{0:T(1024)S(1)} %bitcast.350, s32[]{:T(128)} %constant.29.clone.1), kind=kCustom, calls=%fused_computation.363 | custom fusion | bytes 16388
  108.5 6.1 %fusion.48 = f32[2,8,16,256]{3,2,1,0:T(8,128)} fusion(f32[16,2,8,256]{3,0,2,1:T(8,128)S(1)} %select_bitcast_fusion.1, f32[2,8]{1,0:T(2,128)S(1)} %get-tuple-element.24, f32[2,8,256]{2,1,0:T(8,128)S(1)} %bitcast.314, f32[2,8,256]{2,1,0:T(8,128)S(1)} %bitcast.339, f32[2,8,256]{2,1,0:T(8,128)S(1)} %bitcast.340, f32[2,8,256]{2,1,0:T(8,128)S(1)} %get-tuple-element.66, ...), kind=kOutput, calls=%fused_computation.52 | convolution fusion | flops 211812352 | bytes 606272 | tf_op jit(solution)/shard_map/abij,sabj->sabi/dot_general | solution.py:43
  114.6 1.3 collective-permute-start.6
  115.9 1.3 collective-permute-start.7
  117.2 246.6 %all-reduce.2.cloned.1.call-done = f32[16,64,16]{1,2,0:T(8,128)} async-done(((f32[16,64,16]{1,2,0:T(8,128)}), f32[16,64,16]{1,2,0:T(8,128)}) %all-reduce.2.cloned.1.call-update) | async-done | bytes 65552 | tf_op jit(solution)/shard_map/psum | solution.py:111
  363.8 1.5 convolution_bitcast_fusion.2
  366.1 2.0 reshape.333
  368.1 1.8 convolution_multiply_fusion.13
  369.9 1.7 convolution_multiply_fusion.14
  371.6 1.7 convolution_multiply_fusion.11
  386.3 1.3 fusion.208
  388.5 1.3 collective-permute-start.3
  389.8 4.2 collective-permute-start.2
  394.0 1.1 maximum_maximum_fusion.1
  403.4 1.4 maximum_maximum_fusion
  404.8 6.2 %fusion.60 = f32[2,8,16,256]{3,2,1,0:T(8,128)S(1)} fusion(f32[2,8]{1,0:T(2,128)S(1)} %copy-done.26, f32[2,8,256]{2,1,0:T(8,128)S(1)} %bitcast.334, f32[2,8,256]{2,1,0:T(8,128)S(1)} %bitcast.332, f32[2,8,256]{2,1,0:T(8,128)S(1)} %bitcast.336, f32[2,8,256]{2,1,0:T(8,128)S(1)} %bitcast.315, f32[2,8,256]{2,1,0:T(8,128)S(1)} %get-tuple-element.66, ...), kind=kOutput, calls=%fused_computation.64 | convolution fusion | flops 211812352 | bytes 623616 | tf_op jit(solution)/shard_map/abij,sabj->sabi/dot_general | solution.py:43
  411.1 6.2 %fusion.24 = f32[2,8,16,256]{3,2,1,0:T(8,128)S(1)} fusion(f32[2,8]{1,0:T(2,128)S(1)} %copy-done.25, f32[2,8,256]{2,1,0:T(8,128)S(1)} %bitcast.345, f32[2,8,256]{2,1,0:T(8,128)S(1)} %bitcast.344, f32[2,8,256]{2,1,0:T(8,128)S(1)} %bitcast.343, f32[2,8,256]{2,1,0:T(8,128)S(1)} %bitcast.316, f32[2,8,256]{2,1,0:T(8,128)S(1)} %get-tuple-element.66, ...), kind=kOutput, calls=%fused_computation.28 | convolution fusion | flops 211812352 | bytes 623616 | tf_op jit(solution)/shard_map/abij,sabj->sabi/dot_general | solution.py:43
  417.4 6.3 %fusion.72 = f32[2,8,16,256]{3,2,1,0:T(8,128)S(1)} fusion(f32[2,8]{1,0:T(2,128)S(1)} %copy-done.24, f32[2,8,256]{2,1,0:T(8,128)S(1)} %bitcast.326, f32[2,8,256]{2,1,0:T(8,128)S(1)} %bitcast.329, f32[2,8,256]{2,1,0:T(8,128)S(1)} %bitcast.327, f32[2,8,256]{2,1,0:T(8,128)S(1)} %bitcast.317, f32[2,8,256]{2,1,0:T(8,128)S(1)} %get-tuple-element.66, ...), kind=kOutput, calls=%fused_computation.76 | convolution fusion | flops 211812352 | bytes 623616 | tf_op jit(solution)/shard_map/abij,sabj->sabi/dot_general | solution.py:43
  423.6 6.3 %fusion = f32[2,8,16,256]{3,2,1,0:T(8,128)S(1)} fusion(f32[2,8]{1,0:T(2,128)S(1)} %copy-done.23, f32[2,8,256]{2,1,0:T(8,128)S(1)} %bitcast.348, f32[2,8,256]{2,1,0:T(8,128)S(1)} %bitcast.347, f32[2,8,256]{2,1,0:T(8,128)S(1)} %bitcast.346, f32[2,8,256]{2,1,0:T(8,128)S(1)} %bitcast.318, f32[2,8,256]{2,1,0:T(8,128)S(1)} %get-tuple-element.66, ...), kind=kOutput, calls=%fused_computation.4 | convolution fusion | flops 211812352 | bytes 623616 | tf_op jit(solution)/shard_map/abij,sabj->sabi/dot_general | solution.py:43
  429.9 6.2 %fusion.84 = f32[2,8,16,256]{3,2,1,0:T(8,128)S(1)} fusion(f32[2,8]{1,0:T(2,128)S(1)} %copy-done.22, f32[2,8,256]{2,1,0:T(8,128)S(1)} %bitcast.325, f32[2,8,256]{2,1,0:T(8,128)S(1)} %bitcast.324, f32[2,8,256]{2,1,0:T(8,128)S(1)} %bitcast.323, f32[2,8,256]{2,1,0:T(8,128)S(1)} %bitcast.319, f32[2,8,256]{2,1,0:T(8,128)S(1)} %get-tuple-element.66, ...), kind=kOutput, calls=%fused_computation.88 | convolution fusion | flops 211812352 | bytes 623616 | tf_op jit(solution)/shard_map/abij,sabj->sabi/dot_general | solution.py:43
  436.2 6.2 %fusion.12 = f32[2,8,16,256]{3,2,1,0:T(8,128)S(1)} fusion(f32[2,8]{1,0:T(2,128)S(1)} %copy-done.21, f32[2,8,256]{2,1,0:T(8,128)S(1)} %bitcast.342, f32[2,8,256]{2,1,0:T(8,128)S(1)} %bitcast.341, f32[2,8,256]{2,1,0:T(8,128)S(1)} %bitcast.337, f32[2,8,256]{2,1,0:T(8,128)S(1)} %bitcast.320, f32[2,8,256]{2,1,0:T(8,128)S(1)} %get-tuple-element.66, ...), kind=kOutput, calls=%fused_computation.16 | convolution fusion | flops 211812352 | bytes 623616 | tf_op jit(solution)/shard_map/abij,sabj->sabi/dot_general | solution.py:43
  442.5 6.4 %fusion.205 = f32[2,8,16,256]{3,2,1,0:T(8,128)S(1)} fusion(f32[2,8,16,256]{3,2,1,0:T(8,128)S(1)} %copy-done.29, f32[2,8,16,256]{3,2,1,0:T(8,128)S(1)} %fusion.60, f32[2,8,16,256]{3,2,1,0:T(8,128)S(1)} %fusion.72, f32[2,8,16,256]{3,2,1,0:T(8,128)S(1)} %fusion.84, f32[2,8]{1,0:T(2,128)S(1)} %copy-done.20, f32[2,8,256]{2,1,0:T(8,128)S(1)} %bitcast.328, ...), kind=kOutput, calls=%fused_computation.194 | convolution fusion | flops 212074496 | bytes 1672192 | tf_op jit(solution)/shard_map/abij,sabj->sabi/dot_general | solution.py:43
  449.0 6.4 %fusion.199 = f32[2,8,16,256]{3,2,1,0:T(8,128)S(1)} fusion(f32[2,8,16,256]{3,2,1,0:T(8,128)S(1)} %fusion, f32[2,8,16,256]{3,2,1,0:T(8,128)S(1)} %fusion.12, f32[2,8,16,256]{3,2,1,0:T(8,128)S(1)} %fusion.24, f32[2,8,16,256]{3,2,1,0:T(8,128)S(1)} %fusion.205, f32[2,8]{1,0:T(2,128)S(1)} %copy-done.19, f32[2,8,256]{2,1,0:T(8,128)S(1)} %bitcast.333, ...), kind=kOutput, calls=%fused_computation.192 | convolution fusion | flops 212140032 | bytes 1672192 | tf_op jit(solution)/shard_map/abij,sabj->sabi/dot_general | solution.py:43
  456.7 50.9 %gather_fusion.2 = f32[4096,16]{1,0:T(8,128)} fusion(f32[16,2,8,256]{0,3,2,1:T(8,128)S(1)} %copy.79, s32[4096]{0:T(1024)S(1)} %bitcast.306), kind=kCustom, calls=%fused_computation.1.clone | custom fusion | bytes 573440 | tf_op jit(solution)/shard_map/jit(take_along_axis)/gather | solution.py:117
  507.6 2.2 copy.80
  (165 shorter events, 32.7 us)
Async XLA Ops:
  6.5 56.3 %copy-start = (f32[2,8,64,256]{3,2,1,0:T(8,128)S(1)}, f32[2,8,64,256]{3,2,1,0:T(8,128)}, u32[]{:S(2)}) copy-start(f32[2,8,64,256]{3,2,1,0:T(8,128)} %param.17) | copy-start | bytes 3145732
  6.5 357.3 %all-reduce.2.cloned.1.call-start = ((), (), s32[]{:S(2)}) async-start(), calls=%async_computation | async-start | bytes 262144 | tf_op jit(solution)/shard_map/psum | solution.py:111
  60.6 21.3 %copy-start.4 = (f32[2,8,64,64]{3,2,1,0:T(8,128)S(1)}, f32[2,8,64,64]{3,2,1,0:T(8,128)}, u32[]{:S(2)}) copy-start(f32[2,8,64,64]{3,2,1,0:T(8,128)} %param.18) | copy-start | bytes 786436
  62.9 45.6 %copy-start.1 = (f32[16,2,8,256]{3,0,2,1:T(8,128)}, f32[16,2,8,256]{3,0,2,1:T(8,128)S(1)}, u32[]{:S(2)}) copy-start(f32[16,2,8,256]{3,0,2,1:T(8,128)S(1)} %select_bitcast_fusion.1) | copy-start | bytes 786436
  62.9 21.4 %copy-start.10 = (f32[3,2,8,256]{3,2,1,0:T(8,128)S(1)}, f32[3,2,8,256]{3,2,1,0:T(8,128)}, u32[]{:S(2)}) copy-start(f32[3,2,8,256]{3,2,1,0:T(8,128)} %param.14) | copy-start | bytes 147460
  64.0 26.4 %copy-start.9 = (s32[2,8,256]{2,1,0:T(8,128)S(1)}, s32[2,8,256]{2,1,0:T(8,128)}, u32[]{:S(2)}) copy-start(s32[2,8,256]{2,1,0:T(8,128)} %param.13) | copy-start | bytes 49156
  64.1 26.4 %copy-start.28 = (s32[2]{0:T(128)S(1)}, s32[2]{0:T(128)}, u32[]{:S(2)}) copy-start(s32[2]{0:T(128)} %constant.59) | copy-start | bytes 28
  64.1 26.5 %copy-start.27 = (s32[2]{0:T(128)S(1)}, s32[2]{0:T(128)}, u32[]{:S(2)}) copy-start(s32[2]{0:T(128)} %constant.62) | copy-start | bytes 28
  64.3 41.9 %copy-start.3 = (s32[16,2,8]{0,2,1:T(8,128)S(1)}, s32[16,2,8]{0,2,1:T(8,128)}, u32[]{:S(2)}) copy-start(s32[16,2,8]{0,2,1:T(8,128)} %param.16) | copy-start | bytes 3076
  64.4 42.7 %copy-start.6 = (s32[9,2,8]{0,2,1:T(8,128)S(1)}, s32[9,2,8]{0,2,1:T(8,128)}, u32[]{:S(2)}) copy-start(s32[9,2,8]{0,2,1:T(8,128)} %param.15) | copy-start | bytes 1732
  64.4 43.5 %copy-start.8 = (f32[16,64,64]{2,1,0:T(8,128)S(1)}, f32[16,64,64]{2,1,0:T(8,128)}, u32[]{:S(2)}) copy-start(f32[16,64,64]{2,1,0:T(8,128)} %param.20) | copy-start | bytes 786436
  64.4 50.2 %collective-permute-start.4 = (f32[4,2,8,256]{3,0,2,1:T(4,128)S(1)}, f32[4,2,8,256]{3,0,2,1:T(4,128)S(1)}, u32[]{:S(2)}, u32[]{:S(2)}) collective-permute-start(f32[4,2,8,256]{3,0,2,1:T(4,128)S(1)} %bitcast.310), channel_id=1, source_target_pairs={{0,128},{128,256},{256,384},{384,512},{512,640},{640,768},{768,896... | collective-permute-start | bytes 196616 | tf_op jit(solution)/shard_map/ppermute | solution.py:16
  73.5 41.0 %collective-permute-start.5 = (f32[4,2,8,256]{3,0,2,1:T(4,128)S(1)}, f32[4,2,8,256]{3,0,2,1:T(4,128)S(1)}, u32[]{:S(2)}, u32[]{:S(2)}) collective-permute-start(f32[4,2,8,256]{3,0,2,1:T(4,128)S(1)} %bitcast.311), channel_id=1, source_target_pairs={{128,0},{256,128},{384,256},{512,384},{640,512},{768,640},{896,768... | collective-permute-start | bytes 196616 | tf_op jit(solution)/shard_map/ppermute | solution.py:19
  85.3 302.3 %collective-permute-start = (f32[19,1,8,256]{3,0,2,1:T(8,128)}, f32[19,1,8,256]{3,0,2,1:T(8,128)}, u32[]{:S(2)}, u32[]{:S(2)}) collective-permute-start(f32[19,1,8,256]{3,0,2,1:T(8,128)} %get-tuple-element.59), channel_id=1, source_target_pairs={{0,128},{128,256},{256,384},{384,512},{512,640},{640,768},{768,896... | collective-permute-start | bytes 466952 | tf_op jit(solution)/shard_map/ppermute | solution.py:16
  87.3 300.4 %collective-permute-start.1 = (f32[19,1,8,256]{3,0,2,1:T(8,128)}, f32[19,1,8,256]{3,0,2,1:T(8,128)}, u32[]{:S(2)}, u32[]{:S(2)}) collective-permute-start(f32[19,1,8,256]{3,0,2,1:T(8,128)} %get-tuple-element.60), channel_id=1, source_target_pairs={{128,0},{256,128},{384,256},{512,384},{640,512},{768,640},{896,768... | collective-permute-start | bytes 466952 | tf_op jit(solution)/shard_map/ppermute | solution.py:19
  114.6 250.7 %collective-permute-start.6 = (f32[4,6,2,256]{3,0,2,1:T(4,128)S(1)}, f32[4,6,2,256]{3,0,2,1:T(4,128)S(1)}, u32[]{:S(2)}, u32[]{:S(2)}) collective-permute-start(f32[4,6,2,256]{3,0,2,1:T(4,128)S(1)} %get-tuple-element.63), channel_id=1, source_target_pairs={{0,1},{1,2},{2,3},{3,4},{4,5},{5,6},{6,7},{7,8},{8,9},{9,10},{10,1... | collective-permute-start | bytes 147464 | tf_op jit(solution)/shard_map/ppermute | solution.py:16
  115.9 249.4 %collective-permute-start.7 = (f32[4,6,2,256]{3,0,2,1:T(4,128)S(1)}, f32[4,6,2,256]{3,0,2,1:T(4,128)S(1)}, u32[]{:S(2)}, u32[]{:S(2)}) collective-permute-start(f32[4,6,2,256]{3,0,2,1:T(4,128)S(1)} %get-tuple-element.64), channel_id=1, source_target_pairs={{1,0},{2,1},{3,2},{4,3},{5,4},{6,5},{7,6},{8,7},{9,8},{10,9},{11,1... | collective-permute-start | bytes 147464 | tf_op jit(solution)/shard_map/ppermute | solution.py:19
  368.0 5.3 %copy-start.7 = (f32[16,64,64]{2,1,0:T(8,128)S(1)}, f32[16,64,64]{2,1,0:T(8,128)}, u32[]{:S(2)}) copy-start(f32[16,64,64]{2,1,0:T(8,128)} %param.19) | copy-start | bytes 786436
  378.3 4.0 copy-start.14
  379.3 4.0 copy-start.13
  380.3 4.0 copy-start.12
  383.3 4.4 copy-start.2
  388.5 6.7 %collective-permute-start.3 = (f32[19,4,1,256]{3,0,2,1:T(8,128)S(1)}, f32[19,4,1,256]{3,0,2,1:T(8,128)S(1)}, u32[]{:S(2)}, u32[]{:S(2)}) collective-permute-start(f32[19,4,1,256]{3,0,2,1:T(8,128)S(1)} %get-tuple-element.52), channel_id=1, source_target_pairs={{1,0},{2,1},{3,2},{4,3},{5,4},{6,5},{7,6},{8,7},{9,8},{10,9},{11,1... | collective-permute-start | bytes 233480 | tf_op jit(solution)/shard_map/ppermute | solution.py:19
  389.8 9.3 %collective-permute-start.2 = (f32[19,4,1,256]{3,0,2,1:T(8,128)S(1)}, f32[19,4,1,256]{3,0,2,1:T(8,128)S(1)}, u32[]{:S(2)}, u32[]{:S(2)}) collective-permute-start(f32[19,4,1,256]{3,0,2,1:T(8,128)S(1)} %get-tuple-element.51), channel_id=1, source_target_pairs={{0,1},{1,2},{2,3},{3,4},{4,5},{5,6},{6,7},{7,8},{8,9},{9,10},{10,1... | collective-permute-start | bytes 233480 | tf_op jit(solution)/shard_map/ppermute | solution.py:16
  404.8 6.3 %copy-start.25 = (f32[2,8]{1,0:T(2,128)S(1)}, f32[2,8]{1,0:T(2,128)}, u32[]{:S(2)}) copy-start(f32[2,8]{1,0:T(2,128)} %get-tuple-element.23) | copy-start | bytes 196
  411.1 6.3 %copy-start.24 = (f32[2,8]{1,0:T(2,128)S(1)}, f32[2,8]{1,0:T(2,128)}, u32[]{:S(2)}) copy-start(f32[2,8]{1,0:T(2,128)} %get-tuple-element.26) | copy-start | bytes 196
  417.4 6.3 %copy-start.23 = (f32[2,8]{1,0:T(2,128)S(1)}, f32[2,8]{1,0:T(2,128)}, u32[]{:S(2)}) copy-start(f32[2,8]{1,0:T(2,128)} %get-tuple-element.29) | copy-start | bytes 196
  423.6 6.3 %copy-start.22 = (f32[2,8]{1,0:T(2,128)S(1)}, f32[2,8]{1,0:T(2,128)}, u32[]{:S(2)}) copy-start(f32[2,8]{1,0:T(2,128)} %get-tuple-element.27) | copy-start | bytes 196
  429.9 6.3 %copy-start.21 = (f32[2,8]{1,0:T(2,128)S(1)}, f32[2,8]{1,0:T(2,128)}, u32[]{:S(2)}) copy-start(f32[2,8]{1,0:T(2,128)} %get-tuple-element.30) | copy-start | bytes 196
  436.2 6.3 %copy-start.20 = (f32[2,8]{1,0:T(2,128)S(1)}, f32[2,8]{1,0:T(2,128)}, u32[]{:S(2)}) copy-start(f32[2,8]{1,0:T(2,128)} %get-tuple-element.28) | copy-start | bytes 196
  436.2 6.3 %copy-start.29 = (f32[2,8,16,256]{3,2,1,0:T(8,128)S(1)}, f32[2,8,16,256]{3,2,1,0:T(8,128)}, u32[]{:S(2)}) copy-start(f32[2,8,16,256]{3,2,1,0:T(8,128)} %fusion.48) | copy-start | bytes 786436
  442.5 6.4 %copy-start.19 = (f32[2,8]{1,0:T(2,128)S(1)}, f32[2,8]{1,0:T(2,128)}, u32[]{:S(2)}) copy-start(f32[2,8]{1,0:T(2,128)} %get-tuple-element.22) | copy-start | bytes 196
  (7 other events, 27.5 us)
Sparse Core Ops, SparseCore 0:
  84.4 279.3 all-reduce.1
where the time goes:
time: 521 us; the launch traced here: 517 us
  waiting for transfers between devices  247 us (47%)
  local copies, waits for them, and re-layouts  129 us (25%)
  matrix products  79.2 us (15%)
  starting transfers between devices  30.6 us (6%)
  other arithmetic  16.5 us (3%)
  between operations  15.2 us (3%)
    psum x1, waiting for transfers between devices, on_device(): top = lax.psum(terms, ('row', 'col')).reshape(nodes_count, rank, rhs)  247 us
    dot_general x9, matrix products, near_term(): jnp.einsum('abij,sabj->sabi', tile, values, precision=lax.Precision.HIGHEST)  56.4 us
    gather x2, local copies, waits for them, and re-layouts, on_device(): return jnp.take_along_axis(result, inverse_order(leaf_order)[None], axis=3)  53.1 us
    gather x2, local copies, waits for them, and re-layouts, on_device(): sorted_vec = jnp.take_along_axis(vectors, leaf_order[None], axis=3)  53.1 us
    dot_general x16, matrix products, on_device(): moved = jnp.einsum('jk,ksab->jsab', coupling[slot], window, precision=hp)  18.1 us
    unnamed x94, local copies, waits for them, and re-layouts  17.4 us
    ppermute x4, starting transfers between devices, extended(): lax.ppermute(lax.slice_in_dim(block, block.shape[dim] - width, None, axis...  16.6 us
    ppermute x4, starting transfers between devices, extended(): lax.ppermute(lax.slice_in_dim(block, 0, width, axis=dim), axis, backward)  14 us
  transfers between devices with their start and end apart: 9, of which 1 were waited for; matrix products, arithmetic and copies ran while one was open for 11% of the time, Pallas kernels for 0%

commit v1 on v0

v1 whole, which is shorter than its diff:
```python
import functools

import jax
import jax.numpy as jnp
from jax import lax
from jax.experimental import pallas as pl
from jax.experimental.pallas import tpu as pltpu
from jax.sharding import PartitionSpec as P

F32, BF16 = jnp.float32, jnp.bfloat16
MESH = pl.DeviceIdType.MESH
RHS, LR, LC, LEAF, RANK, TOPN = 16, 2, 8, 256, 64, 16
WIDE = LC + 2
REC = 40
softening = 0.01

NN = (((1,), (0,)), ((), ()))
NT = (((1,), (1,)), ((), ()))
TN = (((0,), (0,)), ((), ()))


def far_offsets():
    return [(i, j) for i in range(-2, 3) for j in range(-2, 3) if max(abs(i), abs(j)) == 2]


def dot(a, b, dims=NN):
    return lax.dot_general(a, b, dims, preferred_element_type=F32)


def split2(x):
    hi = x.astype(BF16)
    return hi, (x - hi.astype(F32)).astype(BF16)


def split3(x):
    a = x.astype(BF16).astype(F32)
    r = x - a
    b = r.astype(BF16).astype(F32)
    return a, b, r - b


def kernel(
    dims,
    vec,
    order,
    off,
    nmask,
    fmask,
    basis,
    transfer,
    coupling,
    topc,
    owner_ref,
    out,
    vin,
    vout,
    io_sem,
    nw,
    cw,
    perm,
    bh,
    bl,
    th,
    tl,
    lead,
    feat,
    qt,
    vhl,
    wf,
    wt,
    gp,
    nacc,
    eh,
    el,
    am,
    send_a,
    recv_a,
    mine_y,
    recv_y,
    mine_z,
    recv_z,
    recv_c,
    nsend,
    nrecv,
    csend,
    crecv,
    asend,
    arecv,
    ysend,
    yrecv,
    zsend,
    zrecv,
    dsend,
    drecv,
):
    nx, nzl, ny, nzh, nc = dims
    rows_n, cols_n = nzh * nc, nx * nzl * ny
    group, nz = nx * nc, nzh * nzl
    row, col = lax.axis_index("row"), lax.axis_index("col")
    zh, core = row // nc, row % nc
    x, zl, y = col // (nzl * ny), (col // ny) % nzl, col % ny
    me_g, me_z = x * nc + core, zh * nzl + zl

    def member(i):
        return (zh * nc + i % nc, (i // nc) * (nzl * ny) + zl * ny + y)

    def along_y(i):
        return (row, x * (nzl * ny) + zl * ny + i)

    def along_z(i):
        return ((i // nzl) * nc + core, x * (nzl * ny) + (i % nzl) * ny + y)

    def beside(dr, dc):
        return ((row + dr + rows_n) % rows_n, (col + dc + cols_n) % cols_n)

    half = [slice(0, 128), slice(128, 256)]
    loads = [pltpu.make_async_copy(vec.at[:, half[h]], vin.at[h], io_sem.at[h]) for h in range(2)]
    for copy in loads:
        copy.start()

    around = [(i, j) for i in (-1, 0, 1) for j in (-1, 0, 1) if (i, j) != (0, 0)]
    barrier = pltpu.get_barrier_semaphore()

    def greet(device):
        pl.semaphore_signal(barrier, inc=1, device_id=device, device_id_type=MESH)

    @pl.loop(1, group)
    def _(i):
        greet(member((me_g + i) % group))

    @pl.loop(1, ny)
    def _(i):
        greet(along_y((y + i) % ny))

    @pl.loop(1, nz)
    def _(i):
        greet(along_z((me_z + i) % nz))

    for step in around:
        greet(beside(*step))

    low_lanes = lax.broadcasted_iota(jnp.int32, (8, 128), 1) < RANK
    low_lanes16 = lax.broadcasted_iota(jnp.int32, (16, 128), 1) < RANK
    owner = owner_ref[0, 0]

    def spread(tile):
        return jnp.concatenate(
            [jnp.where(low_lanes, tile, 0.0), jnp.where(low_lanes, 0.0, tile)], 0
        )

    base = lax.broadcasted_iota(jnp.int32, (LR * LC, LEAF), 0)
    row_first = (row * LR + base // LC).astype(F32)
    col_first = (col * LC + base % LC).astype(F32)
    px = ((row_first + off[0:16, :]) - row_first) - 0.5
    py = ((col_first + off[16:32, :]) - col_first) - 0.5
    pz = 0.25 * off[32:48, :] - 0.125
    pn = (px * px + py * py + pz * pz) + softening
    for r in range(LR):
        first = ((1 + r) * WIDE + 1) * REC + 32
        for h in range(2):
            for c, value in enumerate((px, py, pz, pn)):
                nw[pl.ds(first + 4 * h + c, LC, stride=REC), :] = value[
                    r * LC : (r + 1) * LC, h * 128 : (h + 1) * 128
                ]

    def rec_of(wide):
        return pl.multiple_of(wide * REC, 8)

    @pl.loop(0, LR * LC)
    def _(t):
        k = pl.ds(pl.multiple_of(t * RANK, RANK), RANK)
        bh[k, :], bl[k, :] = split2(basis[k, :])
        th[k, :], tl[k, :] = split2(transfer[k, :])

    for copy in loads:
        copy.wait()
    lane_q = lax.broadcasted_iota(jnp.int32, (LEAF, LEAF), 0)

    def sort_leaf(t):
        hot = jnp.where(lane_q == order[pl.ds(t, 1), :], 1.0, 0.0).astype(BF16)
        perm[t] = hot
        v = jnp.concatenate(
            [vin[h, pl.ds(t, 16, stride=16), :] for h in range(2)], 1
        )
        parts = dot(jnp.concatenate(split2(v), 0), hot)
        wide = (1 + t // LC) * WIDE + 1 + t % LC
        at = rec_of(wide)
        for h in range(2):
            both = parts[:16, h * 128 : (h + 1) * 128] + parts[16:, h * 128 : (h + 1) * 128]
            nw[pl.ds(at + 16 * h, 16), :] = both
        sorted2 = parts.astype(BF16)
        vhl[wide] = sorted2
        k = pl.ds(pl.multiple_of(t * RANK, RANK), RANK)
        both = jnp.concatenate([bh[k, :], bl[k, :]], 0)
        c4 = dot(sorted2, both, NT)
        c2 = c4[:16] + c4[16:]
        c = c2 + pltpu.roll(c2, RANK, 1)
        cw[2 + t // LC, 2 + t % LC] = jnp.where(low_lanes, c[:8], c[8:])
        return c

    @pl.loop(0, LR * LC // 2)
    def _(i):
        c = jnp.where(low_lanes16, sort_leaf(2 * i), sort_leaf(2 * i + 1))
        hi, lo = split2(c)
        lead[:, pl.ds(pl.multiple_of(i * 128, 128), 128)] = jnp.concatenate([hi, lo], 0)

    cl = dot(lead[...], th[...])
    cl = (cl[:16] + cl[16:]) + dot(lead[0:16, :], tl[...])
    packed = jnp.concatenate([cl[:8], cl[8:]], 1)
    slots = TOPN // group
    for g in range(group):
        for s in range(slots):
            send_a[g, 8 * s : 8 * s + 8, :] = jnp.where(owner == g * slots + s, packed, 0.0)

    def near_copies():
        found = []
        for n, (dr, dc) in enumerate(around):
            rs = {-1: [1], 0: [1, 2], 1: [2]}[dr]
            c0, count = {-1: (1, 1), 0: (1, LC), 1: (LC, 1)}[dc]
            for r in rs:
                r_to = r - 2 * dr
                c_to = c0 - LC * dc
                found.append((
                    nw.at[pl.ds((r * WIDE + c0) * REC, count * REC)],
                    nw.at[pl.ds((r_to * WIDE + c_to) * REC, count * REC)],
                    (dr, dc),
                ))
        return [
            pltpu.make_async_remote_copy(
                a, b, nsend.at[n], nrecv.at[n], device_id=beside(*s), device_id_type=MESH
            )
            for n, (a, b, s) in enumerate(found)
        ]

    def coef_copies():
        found = []
        for dr, dc in around:
            c0, count = {-1: (2, 2), 0: (2, LC), 1: (LC, 2)}[dc]
            r_to, c_to = 2 - 2 * dr, c0 - LC * dc
            found.append((
                cw.at[2:4, c0 : c0 + count],
                cw.at[r_to : r_to + 2, c_to : c_to + count],
                (dr, dc),
            ))
        return [
            pltpu.make_async_remote_copy(
                a, b, csend.at[n], crecv.at[n], device_id=beside(*s), device_id_type=MESH
            )
            for n, (a, b, s) in enumerate(found)
        ]

    def copy_a(i):
        to = (me_g + i) % group
        return pltpu.make_async_remote_copy(
            send_a.at[to], recv_a.at[i], asend.at[i], arecv.at[i],
            device_id=member(to), device_id_type=MESH,
        )

    def copy_y(i):
        return pltpu.make_async_remote_copy(
            mine_y, recv_y.at[i], ysend.at[i], yrecv.at[i],
            device_id=along_y((y + i) % ny), device_id_type=MESH,
        )

    def copy_z(i):
        return pltpu.make_async_remote_copy(
            mine_z, recv_z.at[i], zsend.at[i], zrecv.at[i],
            device_id=along_z((me_z + i) % nz), device_id_type=MESH,
        )

    def copy_c(i):
        return pltpu.make_async_remote_copy(
            recv_c.at[0], recv_c.at[i], dsend.at[i], drecv.at[i],
            device_id=member((me_g + i) % group), device_id_type=MESH,
        )

    def every(count, copy, act):
        @pl.loop(1, count)
        def _(i):
            act(copy(i))

    start, arrived, left = (lambda c: c.start()), (lambda c: c.wait_recv()), (lambda c: c.wait_send())

    pl.semaphore_wait(barrier, (group - 1) + (ny - 1) + (nz - 1) + len(around))
    every(group, copy_a, start)
    for copy in near_copies():
        copy.start()
    for copy in coef_copies():
        copy.start()

    lane_row = lax.broadcasted_iota(jnp.int32, (8, LEAF), 0)

    def features(wide, own):
        at = rec_of(wide)
        tile = nw[pl.ds(at + 32, 8), :]
        f = jnp.concatenate([tile, pltpu.roll(tile, 4, 0)], 1)
        f = jnp.where(lane_row < 4, f, jnp.where(lane_row == 4, 1.0, 0.0))
        if own is not None:
            feat[own] = f
        a, b, c = split3(f)
        q = jnp.concatenate([a, a, a, b, b, c], 0)
        qt[wide] = jnp.transpose(q).astype(BF16)
        if own is None:
            v = jnp.concatenate([nw[pl.ds(at, 16), :], nw[pl.ds(at + 16, 16), :]], 1)
            vhl[wide] = jnp.concatenate(split2(v), 0)

    @pl.loop(0, LR * LC)
    def _(t):
        features((1 + t // LC) * WIDE + 1 + t % LC, t)

    def near_pair(f, a, b, da, db):
        d = f - jnp.where(lane_row == 0, float(da), jnp.where(lane_row == 1, float(db), 0.0))
        sq = d * d
        m = sq[0:1] + sq[1:2] + sq[2:3]
        d = jnp.where(
            lane_row < 3,
            -2.0 * d,
            jnp.where(lane_row == 3, 1.0, jnp.where(lane_row == 4, m, 0.0)),
        )
        d1, d2, d3 = split3(d)
        p = jnp.concatenate([d1, d2, d3, d1, d2, d1], 0).astype(BF16)
        wide = (1 + a + da) * WIDE + 1 + b + db
        g = lax.rsqrt(dot(qt[wide], p))
        gh, gl = split2(g)
        v = vhl[wide]
        o = dot(v, gh)
        o = (o[:16] + o[16:]) + dot(v[:16], gl)
        r, c = row * LR + a + da, col * LC + b + db
        inside = (r >= 0) & (r < rows_n * LR) & (c >= 0) & (c < cols_n * LC)
        on = nmask[3 * (da + 1) + db + 1, a, b].astype(F32) * jnp.where(inside, 1.0, 0.0)
        return o * on

    def near_group(a, b, das):
        f = feat[a * LC + b]
        total = None
        for da in das:
            for db in (-1, 0, 1):
                term = near_pair(f, a, b, da, db)
                total = term if total is None else total + term
        return total

    def near_own(b):
        nacc[b] = near_group(0, b, (0, 1))
        nacc[LC + b] = near_group(1, b, (-1, 0))

    def near_outer(b):
        nacc[b] += near_group(0, b, (-1,))
        nacc[LC + b] += near_group(1, b, (1,))

    for o in range(0, 16):
        k = slice(o * RANK, (o + 1) * RANK)
        hi, lo = split2(coupling[k, :])
        w = jnp.concatenate([hi, lo], 0)
        wf[o // 2, :, (o % 2) * 128 : (o % 2) * 128 + 128] = jnp.concatenate([w, w], 1)
    for d in range(16):
        k = slice(d * RANK, (d + 1) * RANK)
        hi, lo = split2(topc[k, :])
        w = jnp.concatenate([hi, lo], 0)
        wt[d // 2, :, (d % 2) * 128 : (d % 2) * 128 + 128] = jnp.concatenate([w, w], 1)

    @pl.loop(1, 3)
    def _(b):
        near_own(b)

    every(group, copy_a, arrived)
    total = send_a[me_g]
    for i in range(1, group):
        total = total + recv_a[i]
    mine_y[...] = total
    every(ny, copy_y, start)

    @pl.loop(3, 5)
    def _(b):
        near_own(b)

    @pl.loop(0, LR * LC)
    def _(t):
        k = pl.ds(pl.multiple_of(t * RANK, RANK), RANK)
        tt = jnp.transpose(transfer[k, :])
        thi, tlo = split2(tt)
        q = dot(jnp.concatenate([thi, tlo], 0), bh[k, :])
        q = (q[:RANK] + q[RANK:]) + dot(thi, bl[k, :])
        hi, lo = split2(q)
        gp[t] = dot(jnp.concatenate([hi, lo], 0), perm[t], NT).astype(BF16)

    every(ny, copy_y, arrived)
    total = mine_y[...]
    for i in range(1, ny):
        total = total + recv_y[i]
    mine_z[...] = total
    every(nz, copy_z, start)

    @pl.loop(5, 7)
    def _(b):
        near_own(b)

    for copy in near_copies():
        copy.wait_recv()
    for copy in coef_copies():
        copy.wait_recv()
    for r in (0, 3):

        @pl.loop(0, WIDE)
        def _(c):
            features(r * WIDE + c, None)

    for r in (1, 2):
        for c in (0, WIDE - 1):
            features(r * WIDE + c, None)

    @pl.loop(0, 2)
    def _(i):
        near_own(i * (LC - 1))

    every(nz, copy_z, arrived)
    total = mine_z[...]
    for i in range(1, nz):
        total = total + recv_z[i]
    recv_c[0] = total
    every(group, copy_c, start)

    for r in range(LR + 4):

        @pl.loop(0, LC + 4)
        def _(c):
            hi, lo = split2(spread(cw[r, c]))
            eh[r, c] = hi
            el[r, c] = lo

    for o, (da, db) in enumerate(far_offsets()):

        @pl.loop(0, LC)
        def _(b):
            for a in range(LR):
                r, c = row * LR + a + da, col * LC + b + db
                inside = (r >= 0) & (r < rows_n * LR) & (c >= 0) & (c < cols_n * LC)
                on = fmask[o, a, b].astype(F32) * jnp.where(inside, 1.0, 0.0)
                on = jnp.full((16, 128), on, F32).astype(BF16)
                lanes = slice((o % 2) * 128, (o % 2) * 128 + 128)
                at = pl.multiple_of((a * LC + b) * 16, 16)
                am[o // 2, pl.ds(at, 16), lanes] = eh[2 + a + da, 2 + b + db] * on
                am[o // 2, pl.ds(at + 256, 16), lanes] = el[2 + a + da, 2 + b + db] * on

    far = dot(am[0], wf[0], NT)
    for o in range(1, 8):
        far = far + dot(am[o], wf[o], NT)
    far = far[:256] + far[256:]
    far = far + pltpu.roll(far, RANK, 1)
    fh, fl = split2(far)
    eh_far, el_far = fh, fl
    am[0, 0:256, 0:128] = eh_far
    am[0, 256:512, 0:128] = el_far

    @pl.loop(0, LC)
    def _(b):
        near_outer(b)

    @pl.loop(0, LR * LC)
    def _(t):
        k = pl.ds(pl.multiple_of(t * RANK, RANK), RANK)
        at = pl.multiple_of(t * 16, 16)
        f_hi, f_lo = am[0, pl.ds(at, 16), 0:RANK], am[0, pl.ds(at + 256, 16), 0:RANK]
        q = dot(jnp.concatenate([f_hi, f_lo], 0), bh[k, :])
        q = (q[:16] + q[16:]) + dot(f_hi, bl[k, :])
        q = q + nacc[t] * (1.0 / 48.0)
        q = dot(jnp.concatenate(split2(q), 0), perm[t], NT)
        nacc[t] = q[:16] + q[16:]

    every(group, copy_c, arrived)
    acc = None
    for pair in range(8):
        parts = []
        for d in (2 * pair, 2 * pair + 1):
            h = (owner - d + TOPN) % TOPN
            m = (me_g - h // slots + group) % group
            tile = recv_c[m, pl.ds(0, 8), :] if slots == 1 else recv_c[m, pl.ds(pl.multiple_of((h % slots) * 8, 8), 8), :]
            if d == 0:
                tile = jnp.zeros_like(tile)
            parts.append(spread(tile))
        hi, lo = split2(jnp.concatenate(parts, 1))
        term = dot(jnp.concatenate([hi, lo], 0), wt[pair], NT)
        acc = term if acc is None else acc + term
    acc = acc[:16] + acc[16:]
    acc = acc + pltpu.roll(acc, RANK, 1)
    hi, lo = split2(acc)
    zero = jnp.zeros_like(acc)
    dl = jnp.concatenate(
        [hi.astype(F32), jnp.where(low_lanes16, lo.astype(F32), zero)], 0
    ).astype(BF16)

    @pl.loop(0, LR * LC)
    def _(t):
        q = dot(dl, gp[t])
        q = (q[:16] + q[16:]) + nacc[t]
        for h in range(2):
            vout[h, pl.ds(t, 16, stride=16), :] = q[:, h * 128 : (h + 1) * 128]

    stores = [pltpu.make_async_copy(vout.at[h], out.at[:, half[h]], io_sem.at[h]) for h in range(2)]
    for copy in stores:
        copy.start()

    every(group, copy_a, left)
    every(ny, copy_y, left)
    every(nz, copy_z, left)
    every(group, copy_c, left)
    for copy in near_copies():
        copy.wait_send()
    for copy in coef_copies():
        copy.wait_send()
    for copy in stores:
        copy.wait()


def on_device(
    dims,
    vectors,
    leaf_order,
    offsets,
    near_mask,
    far_mask,
    basis,
    transfer,
    coupling,
    top_coupling,
    cluster_owner,
):
    nx, nzl, ny, nzh, nc = dims
    group, nz = nx * nc, nzh * nzl
    slots = TOPN // group
    vmem = pl.BlockSpec(memory_space=pltpu.VMEM)
    smem = pl.BlockSpec(memory_space=pltpu.SMEM)
    dma = pltpu.SemaphoreType.DMA
    result = pl.pallas_call(
        functools.partial(kernel, dims),
        out_shape=jax.ShapeDtypeStruct((RHS * LR * LC, LEAF), F32),
        in_specs=[pl.BlockSpec(memory_space=pl.ANY), vmem, vmem, smem, smem, vmem, vmem, vmem, vmem, smem],
        out_specs=pl.BlockSpec(memory_space=pl.ANY),
        scratch_shapes=[
            pltpu.VMEM((2, 256, 128), F32),
            pltpu.VMEM((2, 256, 128), F32),
            dma((2,)),
            pltpu.VMEM((4 * WIDE * REC, 128), F32),
            pltpu.VMEM((LR + 4, LC + 4, 8, 128), F32),
            pltpu.VMEM((16, LEAF, LEAF), BF16),
            pltpu.VMEM((1024, LEAF), BF16),
            pltpu.VMEM((1024, LEAF), BF16),
            pltpu.VMEM((1024, RANK), BF16),
            pltpu.VMEM((1024, RANK), BF16),
            pltpu.VMEM((32, 1024), BF16),
            pltpu.VMEM((16, 8, LEAF), F32),
            pltpu.VMEM((4 * WIDE, LEAF, 48), BF16),
            pltpu.VMEM((4 * WIDE, 32, LEAF), BF16),
            pltpu.VMEM((8, 128, 256), BF16),
            pltpu.VMEM((8, 128, 256), BF16),
            pltpu.VMEM((16, 128, LEAF), BF16),
            pltpu.VMEM((16, 16, LEAF), F32),
            pltpu.VMEM((LR + 4, LC + 4, 16, 128), BF16),
            pltpu.VMEM((LR + 4, LC + 4, 16, 128), BF16),
            pltpu.VMEM((8, 512, 256), BF16),
            pltpu.VMEM((group, 8 * slots, 128), F32),
            pltpu.VMEM((group, 8 * slots, 128), F32),
            pltpu.VMEM((8 * slots, 128), F32),
            pltpu.VMEM((ny, 8 * slots, 128), F32),
            pltpu.VMEM((8 * slots, 128), F32),
            pltpu.VMEM((nz, 8 * slots, 128), F32),
            pltpu.VMEM((group, 8 * slots, 128), F32),
            dma((10,)),
            dma((10,)),
            dma((8,)),
            dma((8,)),
            dma((group,)),
            dma((group,)),
            dma((ny,)),
            dma((ny,)),
            dma((nz,)),
            dma((nz,)),
            dma((group,)),
            dma((group,)),
        ],
        compiler_params=pltpu.CompilerParams(
            collective_id=0, has_side_effects=True, vmem_limit_bytes=48 << 20
        ),
        name="operator",
    )(
        vectors.reshape(RHS * LR * LC, LEAF),
        leaf_order.reshape(LR * LC, LEAF),
        offsets.reshape(3 * LR * LC, LEAF),
        near_mask,
        far_mask,
        basis.reshape(LR * LC * RANK, LEAF),
        transfer.reshape(LR * LC * RANK, RANK),
        coupling.reshape(16 * RANK, RANK),
        top_coupling.reshape(TOPN * RANK, RANK),
        cluster_owner,
    )
    return result.reshape(RHS, LR, LC, LEAF)


def solution(mesh, dims=(8, 2, 8, 4, 2)):
    in_specs = (
        P(None, "row", "col", None),
        P("row", "col", None),
        P(None, "row", "col", None),
        P(None, "row", "col"),
        P(None, "row", "col"),
        P("row", "col", None, None),
        P("row", "col", None, None),
        P(),
        P(),
        P("row", "col"),
    )
    out_specs = P(None, "row", "col", None)
    return jax.shard_map(
        functools.partial(on_device, dims),
        mesh=mesh,
        in_specs=in_specs,
        out_specs=out_specs,
        check_vma=False,
    )
```

time: 521 us -> 72 us (0.14)
  waiting for transfers between devices: 247 us -> 0 us
  local copies, waits for them, and re-layouts: 129 us -> 7.61 us
  matrix products: 79.2 us -> 0 us
  Pallas kernels: 0 us -> 63.3 us
  starting transfers between devices: 30.6 us -> 0 us
  other arithmetic: 16.5 us -> 0 us
  between operations: 15.2 us -> 0.69 us
    psum x1 -> x0, waiting for transfers between devices: 247 us -> none  [on_device(): top = lax.psum(terms, ('row', 'col')).reshape(nodes_count, rank, rhs)]
    gather x5 -> x0, local copies, waits for them, and re-layouts: 107 us -> none  [the longest x2 53.1 us: on_device(): return jnp.take_along_axis(result, inverse_order(leaf_order)[None], axis=3)]
    dot_general x30 -> x0, matrix products: 79.2 us -> none  [the longest x9 56.4 us: near_term(): jnp.einsum('abij,sabj->sabi', tile, values, precision=lax.Precision.HIGHEST)]
    pallas_call x0 -> x1, Pallas kernels: none -> 63.3 us  [on_device(): pl.pallas_call(functools.partial(kernel, dims), out_shape=jax.ShapeDtypeS...]
    ppermute x8 -> x0, starting transfers between devices: 30.6 us -> none  [the longest x4 16.6 us: extended(): lax.ppermute(lax.slice_in_dim(block, block.shape[dim] - width, None, axis...]
    unnamed x94 -> x19, local copies, waits for them, and re-layouts: 17.4 us -> 7.61 us
    slice x11 -> x0, other arithmetic: 8.73 us -> none  [the longest x9 7.88 us: kernel_block(): diff = target[comp][..., :, None] - source[comp][..., None, :]]
  transfers between devices with their start and end apart: 9 -> 0, of which waited for: 1 -> 0; matrix products, arithmetic and copies ran while one was open for 11% -> 0% of each run, Pallas kernels for 0% -> 0%
where the time goes in v1:
time: 72 us; the launch traced here: 71.6 us
  Pallas kernels  63.3 us (88%)
  local copies, waits for them, and re-layouts  7.61 us (11%)
    pallas_call x1, Pallas kernels, on_device(): pl.pallas_call(functools.partial(kernel, dims), out_shape=jax.ShapeDtypeS...  63.3 us
    unnamed x19, local copies, waits for them, and re-layouts  7.61 us

profile of v1, /device:TPU:1, one launch (start us, length us, event | category | flops | bytes accessed | tf_op | source)
XLA Modules:
  0.0 71.6 jit_solution(3147138702283979028)
XLA Ops:
  0.0 0.0 copy-start.7
  0.0 0.0 copy-start.5
  0.7 0.0 copy-done.7
  0.7 0.1 copy.11.nmask
  0.8 0.8 %copy.12.fmask = s32[16,2,8]{2,1,0:T(2,128)S(1)} copy(s32[16,2,8]{0,2,1:T(8,128)} %param.14) | data formatting | bytes 2048 | tf_op args[4]
  1.6 0.0 copy-done.5
  1.6 0.0 copy-start
  1.6 1.2 %copy-done = f32[2,8,64,256]{3,2,1,0:T(8,128)S(1)} copy-done((f32[2,8,64,256]{3,2,1,0:T(8,128)S(1)}, f32[2,8,64,256]{3,2,1,0:T(8,128)}, u32[]{:S(2)}) %copy-start) | copy-done | bytes 1048600
  2.8 0.0 copy-start.1
  2.8 1.0 %copy-done.1 = f32[2,8,64,64]{3,2,1,0:T(8,128)S(1)} copy-done((f32[2,8,64,64]{3,2,1,0:T(8,128)S(1)}, f32[2,8,64,64]{3,2,1,0:T(8,128)}, u32[]{:S(2)}) %copy-start.1) | copy-done | bytes 262168
  3.8 0.0 copy-start.2
  3.8 1.0 %copy-done.2 = f32[16,64,64]{2,1,0:T(8,128)S(1)} copy-done((f32[16,64,64]{2,1,0:T(8,128)S(1)}, f32[16,64,64]{2,1,0:T(8,128)}, u32[]{:S(2)}) %copy-start.2) | copy-done | bytes 262168
  4.9 0.0 copy-start.3
  4.9 1.0 %copy-done.3 = f32[16,64,64]{2,1,0:T(8,128)S(1)} copy-done((f32[16,64,64]{2,1,0:T(8,128)S(1)}, f32[16,64,64]{2,1,0:T(8,128)}, u32[]{:S(2)}) %copy-start.3) | copy-done | bytes 262168
  5.9 0.0 copy-start.4
  5.9 0.9 %copy-done.4 = f32[16,2,8,256]{3,2,1,0:T(8,128)S(1)} copy-done((f32[16,2,8,256]{3,2,1,0:T(8,128)S(1)}, f32[16,2,8,256]{3,2,1,0:T(8,128)}, u32[]{:S(2)}) %copy-start.4) | copy-done | bytes 262168
  6.9 0.0 copy-start.6
  6.9 0.7 copy-done.6
  7.6 63.3 %operator.1 = f32[256,256]{1,0:T(8,128)S(1)} custom-call(f32[256,256]{1,0:T(8,128)S(1)} %bitcast.13, s32[16,256]{1,0:T(8,128)S(1)} %bitcast.15, f32[48,256]{1,0:T(8,128)S(1)} %bitcast.14, s32[9,2,8]{2,1,0:T(2,128)S(1)} %copy.11.nmask, s32[16,2,8]{2,1,0:T(2,128)S(1)} %copy.12.fmask, f32[1024,256]{1,0:T(8,128)S(1)} %bitcast.9, f32[1024,64]{1,0:T(8,128)S(1)} %bitcast.10, ...), custom_call_target="tpu_custom_call" | custom-call | tf_op jit(solution)/shard_map/operator/pallas_call | solution.py:533
  70.9 0.7 copy.15
Async XLA Ops:
  0.0 0.7 copy-start.7
  0.0 1.6 %copy-start.5 = (f32[3,2,8,256]{3,2,1,0:T(8,128)S(1)}, f32[3,2,8,256]{3,2,1,0:T(8,128)}, u32[]{:S(2)}) copy-start(f32[3,2,8,256]{3,2,1,0:T(8,128)} %param.12) | copy-start | bytes 147460
  1.6 1.2 %copy-start = (f32[2,8,64,256]{3,2,1,0:T(8,128)S(1)}, f32[2,8,64,256]{3,2,1,0:T(8,128)}, u32[]{:S(2)}) copy-start(f32[2,8,64,256]{3,2,1,0:T(8,128)} %param.15) | copy-start | bytes 3145732
  2.8 1.0 %copy-start.1 = (f32[2,8,64,64]{3,2,1,0:T(8,128)S(1)}, f32[2,8,64,64]{3,2,1,0:T(8,128)}, u32[]{:S(2)}) copy-start(f32[2,8,64,64]{3,2,1,0:T(8,128)} %param.16) | copy-start | bytes 786436
  3.8 1.0 %copy-start.2 = (f32[16,64,64]{2,1,0:T(8,128)S(1)}, f32[16,64,64]{2,1,0:T(8,128)}, u32[]{:S(2)}) copy-start(f32[16,64,64]{2,1,0:T(8,128)} %param.17) | copy-start | bytes 786436
  4.9 1.0 %copy-start.3 = (f32[16,64,64]{2,1,0:T(8,128)S(1)}, f32[16,64,64]{2,1,0:T(8,128)}, u32[]{:S(2)}) copy-start(f32[16,64,64]{2,1,0:T(8,128)} %param.18) | copy-start | bytes 786436
  5.9 0.9 %copy-start.4 = (f32[16,2,8,256]{3,2,1,0:T(8,128)S(1)}, f32[16,2,8,256]{3,2,1,0:T(8,128)}, u32[]{:S(2)}) copy-start(f32[16,2,8,256]{3,2,1,0:T(8,128)} %param.10) | copy-start | bytes 786436
  6.9 0.7 %copy-start.6 = (s32[2,8,256]{2,1,0:T(8,128)S(1)}, s32[2,8,256]{2,1,0:T(8,128)}, u32[]{:S(2)}) copy-start(s32[2,8,256]{2,1,0:T(8,128)} %param.11) | copy-start | bytes 49156

commit v2 on v1

v2 whole, which is shorter than its diff:
```python
import functools

import jax
import jax.numpy as jnp
from jax import lax
from jax.experimental import pallas as pl
from jax.experimental.pallas import tpu as pltpu
from jax.sharding import PartitionSpec as P

F32, BF16 = jnp.float32, jnp.bfloat16
MESH = pl.DeviceIdType.MESH
RHS, LR, LC, LEAF, RANK, TOPN = 16, 2, 8, 256, 64, 16
WIDE = LC + 2
REC = 40
softening = 0.01

CHUNKS = 4
UNROLL = LR * LC // CHUNKS
AHEAD = 3
PLAN = dict(enter=("wfng", ""), a=("m", "wfm"), y=("h", "h"), z=("la", "la"), c=("ebr", "ngebr"))

NN = (((1,), (0,)), ((), ()))
NT = (((1,), (1,)), ((), ()))
TN = (((0,), (0,)), ((), ()))


def far_offsets():
    return [(i, j) for i in range(-2, 3) for j in range(-2, 3) if max(abs(i), abs(j)) == 2]


def dot(a, b, dims=NN):
    return lax.dot_general(a, b, dims, preferred_element_type=F32)


def split2(x):
    hi = x.astype(BF16)
    return hi, (x - hi.astype(F32)).astype(BF16)


def split3(x):
    a = x.astype(BF16).astype(F32)
    r = x - a
    b = r.astype(BF16).astype(F32)
    return a, b, r - b


def kernel(
    dims,
    vec,
    order_in,
    off_in,
    nmask_in,
    fmask_in,
    basis_in,
    transfer_in,
    coupling_in,
    topc_in,
    owner_in,
    out,
    vin,
    vout,
    order,
    off,
    basis,
    transfer,
    coupling,
    topc,
    nmask,
    fmask,
    owner_ref,
    io_sem,
    nw,
    cw,
    perm,
    bh,
    bl,
    th,
    tl,
    lead,
    feat,
    qt,
    vhl,
    wf,
    wt,
    gp,
    nacc,
    eh,
    el,
    am,
    send_a,
    recv_a,
    mine_y,
    recv_y,
    mine_z,
    recv_z,
    recv_c,
    nsend,
    nrecv,
    csend,
    crecv,
    asend,
    arecv,
    ysend,
    yrecv,
    zsend,
    zrecv,
    dsend,
    drecv,
):
    nx, nzl, ny, nzh, nc = dims
    rows_n, cols_n = nzh * nc, nx * nzl * ny
    group, nz = nx * nc, nzh * nzl
    row, col = lax.axis_index("row"), lax.axis_index("col")
    zh, core = row // nc, row % nc
    x, zl, y = col // (nzl * ny), (col // ny) % nzl, col % ny
    me_g, me_z = x * nc + core, zh * nzl + zl

    def member(i):
        return (zh * nc + i % nc, (i // nc) * (nzl * ny) + zl * ny + y)

    def along_y(i):
        return (row, x * (nzl * ny) + zl * ny + i)

    def along_z(i):
        return ((i // nzl) * nc + core, x * (nzl * ny) + (i % nzl) * ny + y)

    def beside(dr, dc):
        return ((row + dr + rows_n) % rows_n, (col + dc + cols_n) % cols_n)

    half = [slice(0, 128), slice(128, 256)]
    moves = [
        (order_in, order),
        (vec.at[:, half[0]], vin.at[0]),
        (vec.at[:, half[1]], vin.at[1]),
    ]
    part = LR * LC * RANK // CHUNKS
    moves += [(basis_in.at[pl.ds(n * part, part)], basis.at[pl.ds(n * part, part)]) for n in range(CHUNKS)]
    late = len(moves)
    moves += [
        (off_in, off),
        (transfer_in, transfer),
        (owner_in, owner_ref),
        (nmask_in, nmask),
        (fmask_in, fmask),
        (topc_in, topc),
        (coupling_in, coupling),
    ]
    loads = [pltpu.make_async_copy(a, b, io_sem.at[n]) for n, (a, b) in enumerate(moves)]
    for copy in loads:
        copy.start()

    around = [(i, j) for i in (-1, 0, 1) for j in (-1, 0, 1) if (i, j) != (0, 0)]
    barrier = pltpu.get_barrier_semaphore()

    def greet(device):
        pl.semaphore_signal(barrier, inc=1, device_id=device, device_id_type=MESH)

    @pl.loop(1, group)
    def _(i):
        greet(member((me_g + i) % group))

    @pl.loop(1, ny)
    def _(i):
        greet(along_y((y + i) % ny))

    @pl.loop(1, nz)
    def _(i):
        greet(along_z((me_z + i) % nz))

    for step in around:
        greet(beside(*step))

    nacc[...] = jnp.zeros_like(nacc)
    low_lanes = lax.broadcasted_iota(jnp.int32, (8, 128), 1) < RANK
    low_lanes16 = lax.broadcasted_iota(jnp.int32, (16, 128), 1) < RANK

    def spread(tile):
        return jnp.concatenate(
            [jnp.where(low_lanes, tile, 0.0), jnp.where(low_lanes, 0.0, tile)], 0
        )

    def rec_of(wide):
        return pl.multiple_of(wide * REC, 8)

    for n in range(3):
        loads[n].wait()
    lane_q = lax.broadcasted_iota(jnp.int32, (LEAF, LEAF), 0)

    def sort_leaf(t):
        hot = jnp.where(lane_q == order[pl.ds(t, 1), :], 1.0, 0.0).astype(BF16)
        perm[t] = hot
        v = jnp.concatenate(
            [vin[h, pl.ds(t, 16, stride=16), :] for h in range(2)], 1
        )
        parts = dot(jnp.concatenate(split2(v), 0), hot)
        wide = (1 + t // LC) * WIDE + 1 + t % LC
        at = rec_of(wide)
        for h in range(2):
            both = parts[:16, h * 128 : (h + 1) * 128] + parts[16:, h * 128 : (h + 1) * 128]
            nw[pl.ds(at + 16 * h, 16), :] = both
        sorted2 = parts.astype(BF16)
        vhl[wide] = sorted2
        k = pl.ds(pl.multiple_of(t * RANK, RANK), RANK)
        hi, lo = split2(basis[k, :])
        bh[k, :], bl[k, :] = hi, lo
        c4 = dot(sorted2, jnp.concatenate([hi, lo], 0), NT)
        c2 = c4[:16] + c4[16:]
        c = c2 + pltpu.roll(c2, RANK, 1)
        cw[2 + t // LC, 2 + t % LC] = jnp.where(low_lanes, c[:8], c[8:])
        return c

    @pl.loop(0, CHUNKS)
    def _(i):
        rows = pl.ds(pl.multiple_of(i * part, part), part)
        pltpu.make_async_copy(basis_in.at[rows], basis.at[rows], io_sem.at[3 + i]).wait()
        cs = [sort_leaf(UNROLL * i + n) for n in range(UNROLL)]
        for n in range(0, UNROLL, 2):
            hi, lo = split2(jnp.where(low_lanes16, cs[n], cs[n + 1]))
            at = pl.multiple_of(i * (UNROLL * RANK) + n * RANK, 128)
            lead[:, pl.ds(at, 128)] = jnp.concatenate([hi, lo], 0)

    loads[late + 1].wait()
    loads[late + 2].wait()
    owner = owner_ref[0, 0]
    th[...], tl[...] = split2(transfer[...])
    cl = dot(lead[...], th[...])
    cl = (cl[:16] + cl[16:]) + dot(lead[0:16, :], tl[...])
    packed = jnp.concatenate([cl[:8], cl[8:]], 1)
    slots = TOPN // group
    for g in range(group):
        for s in range(slots):
            send_a[g, 8 * s : 8 * s + 8, :] = jnp.where(owner == g * slots + s, packed, 0.0)

    loads[late].wait()
    base = lax.broadcasted_iota(jnp.int32, (LR * LC, LEAF), 0)
    row_first = (row * LR + base // LC).astype(F32)
    col_first = (col * LC + base % LC).astype(F32)
    px = ((row_first + off[0:16, :]) - row_first) - 0.5
    py = ((col_first + off[16:32, :]) - col_first) - 0.5
    pz = 0.25 * off[32:48, :] - 0.125
    pn = (px * px + py * py + pz * pz) + softening
    for r in range(LR):
        first = ((1 + r) * WIDE + 1) * REC + 32
        for h in range(2):
            for c, value in enumerate((px, py, pz, pn)):
                nw[pl.ds(first + 4 * h + c, LC, stride=REC), :] = value[
                    r * LC : (r + 1) * LC, h * 128 : (h + 1) * 128
                ]

    def near_copies():
        found = []
        for n, (dr, dc) in enumerate(around):
            rs = {-1: [1], 0: [1, 2], 1: [2]}[dr]
            c0, count = {-1: (1, 1), 0: (1, LC), 1: (LC, 1)}[dc]
            for r in rs:
                r_to = r - 2 * dr
                c_to = c0 - LC * dc
                found.append((
                    nw.at[pl.ds((r * WIDE + c0) * REC, count * REC)],
                    nw.at[pl.ds((r_to * WIDE + c_to) * REC, count * REC)],
                    (dr, dc),
                ))
        return [
            pltpu.make_async_remote_copy(
                a, b, nsend, nrecv, device_id=beside(*s), device_id_type=MESH
            )
            for n, (a, b, s) in enumerate(found)
        ]

    def coef_copies():
        found = []
        for dr, dc in around:
            c0, count = {-1: (2, 2), 0: (2, LC), 1: (LC, 2)}[dc]
            r_to, c_to = 2 - 2 * dr, c0 - LC * dc
            found.append((
                cw.at[2:4, c0 : c0 + count],
                cw.at[r_to : r_to + 2, c_to : c_to + count],
                (dr, dc),
            ))
        return [
            pltpu.make_async_remote_copy(
                a, b, csend, crecv, device_id=beside(*s), device_id_type=MESH
            )
            for n, (a, b, s) in enumerate(found)
        ]

    def copy_a(i):
        to = (me_g + i) % group
        return pltpu.make_async_remote_copy(
            send_a.at[to], recv_a.at[i], asend, arecv,
            device_id=member(to), device_id_type=MESH,
        )

    def copy_y(i):
        return pltpu.make_async_remote_copy(
            mine_y, recv_y.at[i], ysend, yrecv,
            device_id=along_y((y + i) % ny), device_id_type=MESH,
        )

    def copy_z(i):
        return pltpu.make_async_remote_copy(
            mine_z, recv_z.at[i], zsend, zrecv,
            device_id=along_z((me_z + i) % nz), device_id_type=MESH,
        )

    def copy_c(i):
        return pltpu.make_async_remote_copy(
            recv_c.at[0], recv_c.at[i], dsend, drecv,
            device_id=member((me_g + i) % group), device_id_type=MESH,
        )

    def sent(copy, count):
        for i in sorted(range(1, count), key=lambda i: abs(2 * i - count)):
            copy(i).start()

    def done(sem, ref):
        pltpu.make_async_copy(ref, ref, sem).wait()

    near_bytes = nw.at[pl.ds(0, (4 * WIDE - LR * LC) * REC)]
    coef_bytes = nw.at[pl.ds(0, ((LR + 4) * (LC + 4) - LR * LC) * 8)]
    member_bytes = recv_a.at[pl.ds(1, group - 1)]
    y_bytes = recv_y.at[pl.ds(1, ny - 1)]
    z_bytes = recv_z.at[pl.ds(1, nz - 1)]

    lane_row = lax.broadcasted_iota(jnp.int32, (8, LEAF), 0)

    def inside(r, c):
        r, c = row * LR + r, col * LC + c
        ok = (r >= 0) & (r < rows_n * LR) & (c >= 0) & (c < cols_n * LC)
        return jnp.where(ok, 1.0, 0.0)

    def features(wide, own):
        at = rec_of(wide)
        tile = nw[pl.ds(at + 32, 8), :]
        f = jnp.concatenate([tile, pltpu.roll(tile, 4, 0)], 1)
        f = jnp.where(lane_row < 4, f, jnp.where(lane_row == 4, 1.0, 0.0))
        if own is not None:
            feat[own] = f
        a, b, c = split3(f)
        q = jnp.concatenate([a, a, a, b, b, c], 0)
        qt[wide] = jnp.transpose(q).astype(BF16)
        if own is None:
            v = jnp.concatenate([nw[pl.ds(at, 16), :], nw[pl.ds(at + 16, 16), :]], 1)
            v = v * inside(wide // WIDE - 1, wide % WIDE - 1)
            vhl[wide] = jnp.concatenate(split2(v), 0)

    def near_pair(f, a, b, da, db):
        d = f - jnp.where(lane_row == 0, float(da), jnp.where(lane_row == 1, float(db), 0.0))
        sq = d * d
        m = sq[0:1] + sq[1:2] + sq[2:3]
        d = jnp.where(
            lane_row < 3,
            -2.0 * d,
            jnp.where(lane_row == 3, 1.0, jnp.where(lane_row == 4, m, 0.0)),
        )
        d1, d2, d3 = split3(d)
        p = jnp.concatenate([d1, d2, d3, d1, d2, d1], 0).astype(BF16)
        wide = (1 + a + da) * WIDE + 1 + b + db
        g = lax.rsqrt(dot(qt[wide], p))
        gh, gl = split2(g)
        v = vhl[wide]
        o = dot(v, gh)
        o = (o[:16] + o[16:]) + dot(v[:16], gl)
        return o * nmask[a * LC + b, 3 * (da + 1) + db + 1].astype(F32)

    def near_group(a, b, das):
        f = feat[a * LC + b]
        total = None
        for da in das:
            for db in (-1, 0, 1):
                term = near_pair(f, a, b, da, db)
                total = term if total is None else total + term
        return total

    def near_own(b):
        nacc[b] += near_group(0, b, (0, 1))
        nacc[LC + b] += near_group(1, b, (-1, 0))

    def near_outer(b):
        nacc[b] += near_group(0, b, (-1,))
        nacc[LC + b] += near_group(1, b, (1,))

    def weights():
        for n in range(3, 7):
            loads[late + n].wait()
        for w_ref, source in ((wf, coupling), (wt, topc)):

            @pl.loop(0, 8)
            def _(n):
                for m in range(2):
                    k = pl.ds(pl.multiple_of(n * (2 * RANK) + m * RANK, RANK), RANK)
                    w = jnp.concatenate(split2(source[k, :]), 0)
                    w_ref[n, :, m * 128 : (m + 1) * 128] = jnp.concatenate([w, w], 1)

    def own_features():
        @pl.loop(0, LR * LC // 4)
        def _(i):
            for t in (4 * i, 4 * i + 1, 4 * i + 2, 4 * i + 3):
                features((1 + t // LC) * WIDE + 1 + t % LC, t)

    def near_inner(low, high):
        @pl.loop(low, high)
        def _(b):
            near_own(b)

    def carried():
        @pl.loop(0, LR * LC // 2)
        def _(i):
            for t in (2 * i, 2 * i + 1):
                k = pl.ds(pl.multiple_of(t * RANK, RANK), RANK)
                thi, tlo = split2(jnp.transpose(transfer[k, :]))
                q = dot(jnp.concatenate([thi, tlo], 0), bh[k, :])
                q = (q[:RANK] + q[RANK:]) + dot(thi, bl[k, :])
                gp[t] = dot(jnp.concatenate(split2(q), 0), perm[t], NT).astype(BF16)

    def halo_features():
        done(nrecv, near_bytes)

        @pl.loop(0, WIDE // 2)
        def _(i):
            for c in (2 * i, 2 * i + 1):
                for r in (0, 3):
                    features(r * WIDE + c, None)

        for r in (1, 2):
            for c in (0, WIDE - 1):
                features(r * WIDE + c, None)

    def near_ends():
        @pl.loop(0, 2)
        def _(i):
            near_own(i * (LC - 1))

    def near_beyond(low, high):
        @pl.loop(low, high)
        def _(b):
            near_outer(b)

    def far_field():
        done(crecv, coef_bytes)

        @pl.loop(0, LC + 4)
        def _(c):
            for r in range(LR + 4):
                eh[r, c], el[r, c] = split2(spread(cw[r, c] * inside(r - 2, c - 2)))

        @pl.loop(0, LC)
        def _(b):
            for o, (da, db) in enumerate(far_offsets()):
                for a in range(LR):
                    on = fmask[a * LC + b, o].astype(F32)
                    on = jnp.full((16, 128), on, F32).astype(BF16)
                    lanes = slice((o % 2) * 128, (o % 2) * 128 + 128)
                    at = pl.multiple_of((a * LC + b) * 16, 16)
                    am[o // 2, pl.ds(at, 16), lanes] = eh[2 + a + da, 2 + b + db] * on
                    am[o // 2, pl.ds(at + 256, 16), lanes] = el[2 + a + da, 2 + b + db] * on

        far = dot(am[0], wf[0], NT)
        for o in range(1, 8):
            far = far + dot(am[o], wf[o], NT)
        far = far[:256] + far[256:]
        far = far + pltpu.roll(far, RANK, 1)
        fh, fl = split2(far)
        am[0, 0:256, 0:128] = fh
        am[0, 256:512, 0:128] = fl

    def base_result():
        @pl.loop(0, LR * LC // 4)
        def _(i):
            for t in (4 * i, 4 * i + 1, 4 * i + 2, 4 * i + 3):
                k = pl.ds(pl.multiple_of(t * RANK, RANK), RANK)
                at = pl.multiple_of(t * 16, 16)
                f_hi, f_lo = am[0, pl.ds(at, 16), 0:RANK], am[0, pl.ds(at + 256, 16), 0:RANK]
                q = dot(jnp.concatenate([f_hi, f_lo], 0), bh[k, :])
                q = (q[:16] + q[16:]) + dot(f_hi, bl[k, :])
                q = q + nacc[t] * (1.0 / 48.0)
                q = dot(jnp.concatenate(split2(q), 0), perm[t], NT)
                nacc[t] = q[:16] + q[16:]

    blocks = dict(
        w=weights, f=own_features, m=lambda: near_inner(1, LC // 2), n=lambda: near_inner(LC // 2, LC - 1), g=carried, h=halo_features, e=near_ends,
        a=lambda: near_beyond(0, LC // 2), b=lambda: near_beyond(LC // 2, LC), l=far_field, r=base_result,
    )
    ahead = me_z < AHEAD

    def work(slot):
        early, other = PLAN[slot]
        if early == other:
            for name in early:
                blocks[name]()
            return
        for names, which in ((early, ahead), (other, jnp.logical_not(ahead))):
            if names:

                @pl.when(which)
                def _():
                    for name in names:
                        blocks[name]()

    def added(first, others, count):
        terms = [first] + [others[i] for i in range(1, count)]
        while len(terms) > 1:
            terms = [sum(terms[i : i + 2][1:], terms[i]) for i in range(0, len(terms), 2)]
        return terms[0]

    work("enter")
    pl.semaphore_wait(barrier, (group - 1) + (ny - 1) + (nz - 1) + len(around))
    sent(copy_a, group)
    for copy in near_copies():
        copy.start()
    for copy in coef_copies():
        copy.start()
    work("a")
    done(arecv, member_bytes)
    mine_y[...] = added(send_a[me_g], recv_a, group)
    sent(copy_y, ny)
    work("y")
    done(yrecv, y_bytes)
    mine_z[...] = added(mine_y[...], recv_y, ny)
    sent(copy_z, nz)
    work("z")
    done(zrecv, z_bytes)
    recv_c[0] = added(mine_z[...], recv_z, nz)
    sent(copy_c, group)
    work("c")
    done(drecv, member_bytes)
    acc = None
    for pair in range(8):
        parts = []
        for d in (2 * pair, 2 * pair + 1):
            h = (owner - d + TOPN) % TOPN
            m = (me_g - h // slots + group) % group
            tile = recv_c[m, pl.ds(0, 8), :] if slots == 1 else recv_c[m, pl.ds(pl.multiple_of((h % slots) * 8, 8), 8), :]
            if d == 0:
                tile = jnp.zeros_like(tile)
            parts.append(spread(tile))
        hi, lo = split2(jnp.concatenate(parts, 1))
        term = dot(jnp.concatenate([hi, lo], 0), wt[pair], NT)
        acc = term if acc is None else acc + term
    acc = acc[:16] + acc[16:]
    acc = acc + pltpu.roll(acc, RANK, 1)
    hi, lo = split2(acc)
    zero = jnp.zeros_like(acc)
    dl = jnp.concatenate(
        [hi.astype(F32), jnp.where(low_lanes16, lo.astype(F32), zero)], 0
    ).astype(BF16)

    for t in range(LR * LC):
        q = dot(dl, gp[t])
        q = (q[:16] + q[16:]) + nacc[t]
        for h in range(2):
            vout[h, pl.ds(t, 16, stride=16), :] = q[:, h * 128 : (h + 1) * 128]

    stores = [pltpu.make_async_copy(vout.at[h], out.at[:, half[h]], io_sem.at[h]) for h in range(2)]
    for copy in stores:
        copy.start()

    done(asend, member_bytes)
    done(ysend, y_bytes)
    done(zsend, z_bytes)
    done(dsend, member_bytes)
    done(nsend, near_bytes)
    done(csend, coef_bytes)
    for copy in stores:
        copy.wait()


def on_device(
    dims,
    vectors,
    leaf_order,
    offsets,
    near_mask,
    far_mask,
    basis,
    transfer,
    coupling,
    top_coupling,
    cluster_owner,
):
    nx, nzl, ny, nzh, nc = dims
    group, nz = nx * nc, nzh * nzl
    slots = TOPN // group
    hbm = pl.BlockSpec(memory_space=pltpu.HBM)
    dma = pltpu.SemaphoreType.DMA
    result = pl.pallas_call(
        functools.partial(kernel, dims),
        out_shape=jax.ShapeDtypeStruct((RHS * LR * LC, LEAF), F32),
        in_specs=[hbm] * 10,
        out_specs=pl.BlockSpec(memory_space=pl.ANY),
        scratch_shapes=[
            pltpu.VMEM((2, 256, 128), F32),
            pltpu.VMEM((2, 256, 128), F32),
            pltpu.VMEM((LR * LC, LEAF), jnp.int32),
            pltpu.VMEM((3 * LR * LC, LEAF), F32),
            pltpu.VMEM((1024, LEAF), F32),
            pltpu.VMEM((1024, RANK), F32),
            pltpu.VMEM((1024, RANK), F32),
            pltpu.VMEM((1024, RANK), F32),
            pltpu.SMEM((LR * LC, 9), jnp.int32),
            pltpu.SMEM((LR * LC, 16), jnp.int32),
            pltpu.SMEM((1, 1), jnp.int32),
            dma((10 + CHUNKS,)),
            pltpu.VMEM((4 * WIDE * REC, 128), F32),
            pltpu.VMEM((LR + 4, LC + 4, 8, 128), F32),
            pltpu.VMEM((16, LEAF, LEAF), BF16),
            pltpu.VMEM((1024, LEAF), BF16),
            pltpu.VMEM((1024, LEAF), BF16),
            pltpu.VMEM((1024, RANK), BF16),
            pltpu.VMEM((1024, RANK), BF16),
            pltpu.VMEM((32, 1024), BF16),
            pltpu.VMEM((16, 8, LEAF), F32),
            pltpu.VMEM((4 * WIDE, LEAF, 48), BF16),
            pltpu.VMEM((4 * WIDE, 32, LEAF), BF16),
            pltpu.VMEM((8, 128, 256), BF16),
            pltpu.VMEM((8, 128, 256), BF16),
            pltpu.VMEM((16, 128, LEAF), BF16),
            pltpu.VMEM((16, 16, LEAF), F32),
            pltpu.VMEM((LR + 4, LC + 4, 16, 128), BF16),
            pltpu.VMEM((LR + 4, LC + 4, 16, 128), BF16),
            pltpu.VMEM((8, 512, 256), BF16),
            pltpu.VMEM((group, 8 * slots, 128), F32),
            pltpu.VMEM((group, 8 * slots, 128), F32),
            pltpu.VMEM((8 * slots, 128), F32),
            pltpu.VMEM((ny, 8 * slots, 128), F32),
            pltpu.VMEM((8 * slots, 128), F32),
            pltpu.VMEM((nz, 8 * slots, 128), F32),
            pltpu.VMEM((group, 8 * slots, 128), F32),
            *[dma(())] * 12,
        ],
        compiler_params=pltpu.CompilerParams(
            collective_id=0, has_side_effects=True, vmem_limit_bytes=67000000
        ),
        name="operator",
    )(
        vectors.reshape(RHS * LR * LC, LEAF),
        leaf_order.reshape(LR * LC, LEAF),
        offsets.reshape(3 * LR * LC, LEAF),
        near_mask.transpose(1, 2, 0).reshape(LR * LC, 9),
        far_mask.transpose(1, 2, 0).reshape(LR * LC, 16),
        basis.reshape(LR * LC * RANK, LEAF),
        transfer.reshape(LR * LC * RANK, RANK),
        coupling.reshape(16 * RANK, RANK),
        top_coupling.reshape(TOPN * RANK, RANK),
        cluster_owner,
    )
    return result.reshape(RHS, LR, LC, LEAF)


def solution(mesh, dims=(8, 2, 8, 4, 2)):
    in_specs = (
        P(None, "row", "col", None),
        P("row", "col", None),
        P(None, "row", "col", None),
        P(None, "row", "col"),
        P(None, "row", "col"),
        P("row", "col", None, None),
        P("row", "col", None, None),
        P(),
        P(),
        P("row", "col"),
    )
    out_specs = P(None, "row", "col", None)
    return jax.shard_map(
        functools.partial(on_device, dims),
        mesh=mesh,
        in_specs=in_specs,
        out_specs=out_specs,
        check_vma=False,
    )
```

time: 72 us -> 49.4 us (0.69)
  the two profiles are of different devices: /device:TPU:1 before, /device:TPU:384 now
where the time goes in v2:
time: 49.4 us; the launch traced here: 49.2 us
  Pallas kernels  46.9 us (95%)
  local copies, waits for them, and re-layouts  1.67 us (3%)
  between operations  0.66 us (1%)
    pallas_call x1, Pallas kernels, on_device(): pl.pallas_call(functools.partial(kernel, dims), out_shape=jax.ShapeDtypeS...  46.9 us
    unnamed x1, local copies, waits for them, and re-layouts  1.67 us

profile of v2, /device:TPU:384, one launch (start us, length us, event | category | flops | bytes accessed | tf_op | source)
XLA Modules:
  0.0 49.2 jit_solution(7324207573243677937)
XLA Ops:
  0.7 46.9 %operator.1 = f32[256,256]{1,0:T(8,128)} custom-call(f32[256,256]{1,0:T(8,128)} %bitcast.19, s32[16,256]{1,0:T(8,128)} %bitcast.21, f32[48,256]{1,0:T(8,128)} %bitcast.20, s32[16,9]{1,0:T(8,128)} %bitcast.22, s32[16,16]{1,0:T(8,128)} %bitcast.23, f32[1024,256]{1,0:T(8,128)} %bitcast.14, f32[1024,64]{1,0:T(8,128)} %bitcast.16, f32[1024,64]{1,0:T(8,128)} %bitcast.17, ...), custom_call_target="tpu_custom_call" | custom-call | tf_op jit(solution)/shard_map/operator/pallas_call | solution.py:586
  47.5 1.7 %copy.13 = f32[16,2,8,256]{3,2,1,0:T(8,128)} copy(f32[16,2,8,256]{3,2,1,0:T(8,128)} %bitcast.15) | data formatting | bytes 524288

commit v3 on v2

--- a/solution.py
+++ b/solution.py
@@ -17,7 +17,7 @@
 CHUNKS = 4
 UNROLL = LR * LC // CHUNKS
 AHEAD = 3
-PLAN = dict(enter=("wfng", ""), a=("m", "wfm"), y=("h", "h"), z=("la", "la"), c=("ebr", "ngebr"))
+PLAN = dict(enter=("wfng", ""), a=("m", "wfg"), y=("h", "m"), z=("la", "hla"), c=("ebr", "nebr"))
 
 NN = (((1,), (0,)), ((), ()))
 NT = (((1,), (1,)), ((), ()))

time: 49.4 us -> 48.3 us (0.978)
  the two profiles are of different devices: /device:TPU:384 before, /device:TPU:1 now
where the time goes in v3:
time: 48.3 us; the launch traced here: 48.1 us
  Pallas kernels  45.8 us (95%)
  local copies, waits for them, and re-layouts  1.67 us (3%)
  between operations  0.66 us (1%)
    pallas_call x1, Pallas kernels, on_device(): pl.pallas_call(functools.partial(kernel, dims), out_shape=jax.ShapeDtypeS...  45.8 us
    unnamed x1, local copies, waits for them, and re-layouts  1.67 us

profile of v3, /device:TPU:1, one launch (start us, length us, event | category | flops | bytes accessed | tf_op | source)
XLA Modules:
  0.0 48.1 jit_solution(1350765152447322453)
XLA Ops:
  0.7 45.8 %operator.1 = f32[256,256]{1,0:T(8,128)} custom-call(f32[256,256]{1,0:T(8,128)} %bitcast.19, s32[16,256]{1,0:T(8,128)} %bitcast.21, f32[48,256]{1,0:T(8,128)} %bitcast.20, s32[16,9]{1,0:T(8,128)} %bitcast.22, s32[16,16]{1,0:T(8,128)} %bitcast.23, f32[1024,256]{1,0:T(8,128)} %bitcast.14, f32[1024,64]{1,0:T(8,128)} %bitcast.16, f32[1024,64]{1,0:T(8,128)} %bitcast.17, ...), custom_call_target="tpu_custom_call" | custom-call | tf_op jit(solution)/shard_map/operator/pallas_call | solution.py:586
  46.4 1.7 %copy.13 = f32[16,2,8,256]{3,2,1,0:T(8,128)} copy(f32[16,2,8,256]{3,2,1,0:T(8,128)} %bitcast.15) | data formatting | bytes 524288
